TPU v7x, 32 devices: a whole 2x2x4 slice. The times are simulated.
32 devices in a mesh: outer: 4 (over z), dev: 8 (over y, x, core).
Axes of the slice: x: 2, y: 2, z: 4, core: 2. Of those that a mesh axis runs over, the one named last changes fastest.
Arguments:
- partials: bfloat16 [32, 8192, 128], P(('outer', 'dev')), may hold values from -6 to 6
- p_old: bfloat16 [8192, 1024], P('dev'), may hold values from -0.0625 to 0.0625
- p_new: bfloat16 [8192, 1024], P('dev'), may hold values from -0.0625 to 0.0625
- weight: float32 [8192, 128], P('dev'), may hold values from -4 to 4
- m_old: float32 [1024, 128], P('dev'), may hold values from -96 to 96
- v_old: float32 [1024, 128], P('dev'), may hold values from 32 to 1280
Outputs:
- new_weight: float32 [8192, 128], P('dev')
- m_new: float32 [1024, 128], P('dev')
- v_new: float32 [1024, 128], P('dev')
All inputs are finite; a program needn't handle non-finite values.
Results may differ from a plain program's by a relative error of at most 0.0012.
Values may be sent and summed in bfloat16 or wider, within the bound.
A program may use at most 128 MiB of HBM per device.

v0:
```python
import jax
import jax.numpy as jnp
from jax import lax
from jax.sharding import PartitionSpec as P

beta_mean = 0.9
beta_square = 0.95
bias_mean = 0.9999734386011124
bias_square = 0.9940794707796659
adam_epsilon = 1e-08
step_scale = 0.5


def on_device(partials, p_old, p_new, weight, m_old, v_old):
    local_grad = partials[0].astype(jnp.float32)
    grad_rows = lax.psum_scatter(local_grad, "dev", scatter_dimension=0, tiled=True)
    basis = p_new.astype(jnp.float32)
    columns = basis
    projected = lax.psum_scatter(
        jnp.dot(columns.T, grad_rows, precision=lax.Precision.HIGHEST),
        "dev",
        scatter_dimension=0,
        tiled=True,
    )
    projected = lax.psum(projected, "outer")
    columns = p_new
    margin_rows = lax.psum_scatter(
        jnp.dot(columns.T, p_old, preferred_element_type=jnp.float32),
        "dev",
        scatter_dimension=0,
        tiled=True,
    )
    first_piece = lax.all_gather(m_old, "dev", axis=0, tiled=True)
    second_piece = lax.all_gather(v_old, "dev", axis=0, tiled=True)
    first = jnp.dot(margin_rows, first_piece, precision=lax.Precision.HIGHEST)
    second = jnp.dot(margin_rows * margin_rows, second_piece, precision=lax.Precision.HIGHEST)
    m_new = beta_mean * first + (1.0 - beta_mean) * projected
    v_new = beta_square * second + (1.0 - beta_square) * projected * projected
    direction = (m_new / bias_mean / (jnp.sqrt(v_new / bias_square) + adam_epsilon)).astype(
        jnp.bfloat16
    )
    columns = p_new
    update = jnp.dot(
        columns,
        lax.all_gather(direction, "dev", axis=0, tiled=True),
        preferred_element_type=jnp.float32,
    )
    new_weight = weight - step_scale * update
    return (new_weight, m_new, v_new)


def solution(mesh):
    in_specs = (
        P(("outer", "dev"), None, None),
        P("dev", None),
        P("dev", None),
        P("dev", None),
        P("dev", None),
        P("dev", None),
    )
    out_specs = (P("dev", None), P("dev", None), P("dev", None))
    return jax.shard_map(
        on_device, mesh=mesh, in_specs=in_specs, out_specs=out_specs, check_vma=False
    )
```

profile of v0, /device:TPU:0, one launch (start us, length us, event | category | flops | bytes accessed | tf_op | source)
XLA Modules:
  0.0 216.5 jit_solution(17691967801441322931)
XLA Ops:
  7.2 0.0 copy-start
  7.2 0.0 reduce-scatter.6.cloned.1.call-start
  7.2 3.9 %bitcast_convert_fusion = f32[8192,128]{1,0:T(8,128)} fusion(bf16[1,8192,128]{2,1,0:T(8,128)(2,1)} %param.6), kind=kLoop, calls=%fused_computation | loop fusion | flops 1048576 | bytes 6291456 | tf_op jit(solution)/shard_map/convert_element_type | solution.py:15
  11.2 0.0 reduce-scatter.6.cloned.1.call-update
  11.2 0.0 reduce-scatter.8.cloned.1.call-start
  11.2 54.0 %reduce-scatter.6.cloned.1.call-done = f32[1024,128]{1,0:T(8,128)} async-done(((f32[8192,128]{1,0:T(8,128)}), f32[1024,128]{1,0:T(8,128)}) %reduce-scatter.6.cloned.1.call-update) | async-done | bytes 524304 | tf_op jit(solution)/shard_map/reduce_scatter | solution.py:16
  65.3 0.0 copy-done
  65.3 4.1 %fusion.6 = f32[1024,128]{1,0:T(8,128)} fusion(bf16[1024,1024]{1,0:T(8,128)(2,1)S(1)} %copy-done, f32[1024,128]{1,0:T(8,128)} %reduce-scatter.6.cloned.1.call-done), kind=kOutput, calls=%fused_computation.12 | convolution fusion | flops 1610612736 | bytes 3145728 | tf_op jit(solution)/shard_map/dot_general | solution.py:20
  69.4 0.0 reduce-scatter.8.cloned.1.call-update
  69.5 0.0 reduce-scatter.4.cloned.1.call-start
  69.5 5.9 %fusion.5 = f32[1024,1024]{1,0:T(8,128)} fusion(bf16[1024,1024]{1,0:T(8,128)(2,1)S(1)} %copy-done, bf16[1024,1024]{1,0:T(8,128)(2,1)} %param.7), kind=kOutput, calls=%fused_computation.11 | convolution fusion | flops 2147483648 | bytes 8388608 | tf_op jit(solution)/shard_map/dot_general | solution.py:28
  75.4 0.0 copy-start.2
  75.4 0.0 copy-start.4
  75.4 0.0 copy-start.5
  75.4 0.0 reduce-scatter.4.cloned.1.call-update
  75.5 0.0 all-reduce.2.cloned.1.call-start
  75.5 1.0 copy-done.2
  76.5 1.0 copy.9
  77.5 0.0 copy-done.4
  77.5 9.8 %all_gather.9 = f32[1024,128]{1,0:T(8,128)S(1)} all-gather(f32[128,128]{1,0:T(8,128)S(1)} %copy-done.4), channel_id=1, replica_groups=mesh['outer'=4,'dev'=8] {'dev'}, dimensions={0}, use_global_device_ids=true | all-gather | bytes 589824 | tf_op jit(solution)/shard_map/all_gather | solution.py:33
  87.2 16.5 %reduce-scatter.8.cloned.1.call-done = f32[128,128]{1,0:T(8,128)} async-done(((f32[1024,128]{1,0:T(8,128)}), f32[128,128]{1,0:T(8,128)}) %reduce-scatter.8.cloned.1.call-update) | async-done | bytes 65552 | tf_op jit(solution)/shard_map/reduce_scatter | solution.py:19
  103.7 0.0 all-reduce.2.cloned.1.call-update
  103.7 0.0 copy-done.5
  103.8 9.8 %all_gather.10 = f32[1024,128]{1,0:T(8,128)S(1)} all-gather(f32[128,128]{1,0:T(8,128)S(1)} %copy-done.5), channel_id=1, replica_groups=mesh['outer'=4,'dev'=8] {'dev'}, dimensions={0}, use_global_device_ids=true | all-gather | bytes 589824 | tf_op jit(solution)/shard_map/all_gather | solution.py:34
  113.5 44.7 %reduce-scatter.4.cloned.1.call-done = f32[128,1024]{1,0:T(8,128)} async-done(((f32[1024,1024]{1,0:T(8,128)}), f32[128,1024]{1,0:T(8,128)}) %reduce-scatter.4.cloned.1.call-update) | async-done | bytes 524304 | tf_op jit(solution)/shard_map/reduce_scatter | solution.py:27
  158.3 36.5 %all-reduce.2.cloned.1.call-done = f32[128,128]{1,0:T(8,128)} async-done(((f32[128,128]{1,0:T(8,128)}), f32[128,128]{1,0:T(8,128)}) %all-reduce.2.cloned.1.call-update) | async-done | bytes 65552 | tf_op jit(solution)/shard_map/psum | solution.py:25
  194.8 0.0 copy-start.1
  194.8 1.7 fusion.3
  196.5 0.0 copy-start.3
  196.5 2.4 %divide_convert_fusion = (bf16[128,128]{1,0:T(8,128)(2,1)S(1)}, f32[128,128]{1,0:T(8,128)}) fusion(f32[128,128]{1,0:T(8,128)S(1)} %fusion.3, f32[128,128]{1,0:T(8,128)} %all-reduce.2.cloned.1.call-done, f32[1024,128]{1,0:T(8,128)S(1)} %all_gather.10, f32[128,1024]{1,0:T(8,128)} %reduce-scatter.4.cloned.1.call-done), kind=kOutput, calls=%fused_computation.10 | convolution fusion | flops 201605120 | bytes 1277952 | tf_op jit(solution)/shard_map/dot_general | solution.py:36
  198.9 9.2 %all_gather.11 = bf16[1024,128]{1,0:T(8,128)(2,1)S(1)} all-gather(bf16[128,128]{1,0:T(8,128)(2,1)S(1)} %get-tuple-element.6), channel_id=1, replica_groups=mesh['outer'=4,'dev'=8] {'dev'}, dimensions={0}, use_global_device_ids=true | all-gather | bytes 294912 | tf_op jit(solution)/shard_map/all_gather | solution.py:45
  208.1 0.0 copy-done.1
  208.1 0.8 fusion.1
  209.0 0.0 copy-done.3
  209.0 1.0 copy.10
Async XLA Ops:
  7.2 58.1 %copy-start = (bf16[1024,1024]{1,0:T(8,128)(2,1)S(1)}, bf16[1024,1024]{1,0:T(8,128)(2,1)}, u32[]{:S(2)}) copy-start(bf16[1024,1024]{1,0:T(8,128)(2,1)} %param.8) | copy-start | bytes 6291460
  7.2 58.1 %reduce-scatter.6.cloned.1.call-start = ((), (), s32[]{:S(2)}) async-start(), calls=%async_computation.4 | async-start | bytes 4718592 | tf_op jit(solution)/shard_map/reduce_scatter | solution.py:16
  11.2 92.5 %reduce-scatter.8.cloned.1.call-start = ((), (), s32[]{:S(2)}) async-start(), calls=%async_computation.5 | async-start | bytes 589824 | tf_op jit(solution)/shard_map/reduce_scatter | solution.py:19
  69.5 88.8 %reduce-scatter.4.cloned.1.call-start = ((), (), s32[]{:S(2)}) async-start(), calls=%async_computation.3 | async-start | bytes 4718592 | tf_op jit(solution)/shard_map/reduce_scatter | solution.py:27
  75.4 1.0 copy-start.2
  75.4 2.0 copy-start.4
  75.4 28.3 %copy-start.5 = (f32[128,128]{1,0:T(8,128)S(1)}, f32[128,128]{1,0:T(8,128)}, u32[]{:S(2)}) copy-start(f32[128,128]{1,0:T(8,128)} %param.11) | copy-start | bytes 196612
  75.5 119.3 %all-reduce.2.cloned.1.call-start = ((), (), s32[]{:S(2)}) async-start(), calls=%async_computation.6 | async-start | bytes 131072 | tf_op jit(solution)/shard_map/psum | solution.py:25
  194.8 13.4 %copy-start.1 = (f32[1024,128]{0,1:T(8,128)S(1)}, f32[1024,128]{0,1:T(8,128)}, u32[]{:S(2)}) copy-start(f32[1024,128]{0,1:T(8,128)} %copy.9) | copy-start | bytes 1572868
  196.5 12.5 %copy-start.3 = (f32[128,128]{1,0:T(8,128)}, f32[128,128]{1,0:T(8,128)S(1)}, u32[]{:S(2)}) copy-start(f32[128,128]{1,0:T(8,128)S(1)} %fusion.3) | copy-start | bytes 196612
Sparse Core Ops, SparseCore 0:
  11.3 53.8 reduce-scatter.5
  69.6 34.0 reduce-scatter.7
  107.1 51.1 reduce-scatter.3
  160.5 34.2 all-reduce.1
where the time goes:
time: 217 us
  waiting for transfers between devices  152 us (70%)
  blocking collectives  28.8 us (13%)
  matrix products  15 us (7%)
  between operations  13.8 us (6%)
  other arithmetic  3.94 us (2%)
  local copies, waits for them, and re-layouts  2.99 us (1%)
    reduce_scatter x1, waiting for transfers between devices, on_device(): lax.psum_scatter(local_grad, 'dev', scatter_dimension=0, tiled=True)  54 us
    reduce_scatter x1, waiting for transfers between devices, on_device(): lax.psum_scatter(jnp.dot(columns.T, p_old, preferred_element_type=jnp.flo...  44.7 us
    psum x1, waiting for transfers between devices, on_device(): projected = lax.psum(projected, 'outer')  36.5 us
    reduce_scatter x1, waiting for transfers between devices, on_device(): lax.psum_scatter(jnp.dot(columns.T, grad_rows, precision=lax.Precision.HI...  16.5 us
    all_gather x1, blocking collectives, on_device(): second_piece = lax.all_gather(v_old, 'dev', axis=0, tiled=True)  9.79 us
    all_gather x1, blocking collectives, on_device(): first_piece = lax.all_gather(m_old, 'dev', axis=0, tiled=True)  9.77 us
    all_gather x1, blocking collectives, on_device(): lax.all_gather(direction, 'dev', axis=0, tiled=True)  9.25 us
    dot_general x1, matrix products, on_device(): jnp.dot(columns.T, p_old, preferred_element_type=jnp.float32)  5.92 us
  transfers between devices with their start and end apart: 4, of which 4 were waited for; matrix products, arithmetic and copies ran while one was open for 3% of the time, Pallas kernels for 0%

commit v1 on v0

v1 whole, which is shorter than its diff:
```python
import functools

import jax
import jax.numpy as jnp
from jax import lax
from jax.experimental import pallas as pl
from jax.experimental.pallas import tpu as pltpu
from jax.sharding import PartitionSpec as P

beta_mean = 0.9
beta_square = 0.95
bias_mean = 0.9999734386011124
bias_square = 0.9940794707796659
adam_epsilon = 1e-08
step_scale = 0.5

MESH = pl.DeviceIdType.MESH
F32 = jnp.float32
BF16 = jnp.bfloat16


def contract_rows(a, b):
    return lax.dot_general(a, b, (((0,), (0,)), ((), ())), preferred_element_type=F32)


def kernel(
    n_outer,
    n_dev,
    partials,
    p_old,
    p_new,
    weight,
    m_old,
    v_old,
    new_weight,
    m_new,
    v_new,
    grads,
    basis,
    basis_old,
    weights,
    moments,
    margin,
    margin_partner,
    margin_sum,
    margin_in,
    rotated,
    rotated_in,
    projected,
    projected_partner,
    projected_sum,
    projected_in,
    block,
    block_in,
    direction,
    load_sem,
    grad_send,
    grad_recv,
    mom_send,
    mom_recv,
    fwd_send,
    fwd_recv,
    mp_send,
    mp_recv,
    ms_send,
    ms_recv,
    rot_send,
    rot_recv,
    pp_send,
    pp_recv,
    ps_send,
    ps_recv,
    blk_send,
    blk_recv,
    dir_send,
    dir_recv,
):
    z = lax.axis_index("outer")
    d = lax.axis_index("dev")
    n_chip = n_dev // 2
    q = d // 2
    c = d % 2
    partner = q * 2 + 1 - c
    rows, cols = weight.shape
    rank = p_new.shape[1]
    blk = rank // n_dev
    per = n_dev // n_outer

    def remote(src, dst, send, recv, where):
        return pltpu.make_async_remote_copy(
            src_ref=src, dst_ref=dst, send_sem=send, recv_sem=recv, device_id=where, device_id_type=MESH
        )

    barrier = pltpu.get_barrier_semaphore()
    for j in range(1, n_dev):
        pl.semaphore_signal(barrier, inc=1, device_id=(z, lax.rem(d + j, n_dev)), device_id_type=MESH)
    for j in range(1, n_outer):
        pl.semaphore_signal(barrier, inc=1, device_id=(lax.rem(z + j, n_outer), d), device_id_type=MESH)

    load_new = pltpu.make_async_copy(p_new, basis, load_sem.at[0])
    load_new.start()
    load_old = pltpu.make_async_copy(p_old, basis_old, load_sem.at[1])
    load_old.start()
    load_weight = pltpu.make_async_copy(weight, weights, load_sem.at[2])
    load_weight.start()
    load_own = pltpu.make_async_copy(
        partials.at[pl.ds(pl.multiple_of(d * rows, rows), rows)], grads.at[0], load_sem.at[3]
    )
    load_own.start()

    pl.semaphore_wait(barrier, n_dev - 1 + n_outer - 1)

    def moment_copies(k, owner):
        copies = []
        for j in range(1, n_chip):
            to = (z, lax.rem(q + j, n_chip) * 2 + c)
            for i, src in enumerate((m_old, v_old)):
                copies.append(remote(src, moments.at[i, k], mom_send.at[i, k, j], mom_recv.at[i, k], to))
        return copies

    for k in range(per):
        owner = z * per + k

        @pl.when(d == owner)
        def _():
            for copy in moment_copies(k, owner):
                copy.start()
            for i, src in enumerate((m_old, v_old)):
                pltpu.make_async_copy(src, moments.at[i, k], load_sem.at[4 + i]).start()

    grad_copies = []
    for j in range(1, n_dev):
        to = lax.rem(d + j, n_dev)
        copy = remote(
            partials.at[pl.ds(pl.multiple_of(to * rows, rows), rows)],
            grads.at[j],
            grad_send.at[j],
            grad_recv.at[j],
            (z, to),
        )
        copy.start()
        grad_copies.append(copy)

    load_new.wait()
    load_old.wait()
    width = min(rank, 256)
    for s in range(0, rank, width):
        part = contract_rows(basis[:, s : s + width], basis_old[...])
        margin[s // blk : (s + width) // blk] = part.reshape(width // blk, blk, part.shape[1])

    def scatter_start(val, prt, send, recv):
        copies = []
        for j in list(range(1, n_chip)) + [0]:
            k = lax.rem(q + j, n_chip)
            copy = remote(val.at[2 * k + 1 - c], prt.at[j], send.at[j], recv.at[j], (z, partner))
            copy.start()
            copies.append((j, k, copy))
        return copies

    def scatter_middle(pairs, val, prt, tot, arr, send, recv):
        copies = []
        for j, k, pair in pairs:
            pair.wait_recv()
            tot[j] = val[2 * k + c] + prt[j]
            if j:
                copy = remote(tot.at[j], arr.at[j], send.at[j], recv.at[j], (z, 2 * k + c))
                copy.start()
                copies.append((j, copy))
        return copies

    def scatter_end(copies, tot, arr):
        total = tot[0]
        for j, copy in copies:
            copy.wait_recv()
            total = total + arr[j]
        return total

    margin_pairs = scatter_start(margin, margin_partner, mp_send, mp_recv)

    for k in range(per):
        owner = z * per + k
        mine = c == owner % 2

        @pl.when(d == owner)
        def _():
            for i, src in enumerate((m_old, v_old)):
                pltpu.make_async_copy(src, moments.at[i, k], load_sem.at[4 + i]).wait()

        @pl.when(jnp.logical_and(mine, d != owner))
        def _():
            for i, src in enumerate((m_old, v_old)):
                remote(src, moments.at[i, k], mom_send.at[i, k, 0], mom_recv.at[i, k], (z, d)).wait_recv()

        @pl.when(mine)
        def _():
            for i in range(2):
                remote(
                    moments.at[i, k], moments.at[i, k], fwd_send.at[i, k], fwd_recv.at[i, k], (z, partner)
                ).start()

    margin_copies = scatter_middle(
        margin_pairs, margin, margin_partner, margin_sum, margin_in, ms_send, ms_recv
    )

    for k in range(per):
        mine = c == (z * per + k) % 2

        @pl.when(jnp.logical_not(mine))
        def _():
            for i in range(2):
                remote(
                    moments.at[i, k], moments.at[i, k], fwd_send.at[i, k], fwd_recv.at[i, k], (z, partner)
                ).wait_recv()

    margin_rows = scatter_end(margin_copies, margin_sum, margin_in)
    old = moments[...].reshape(2, per * blk, cols)
    rotated[0] = jnp.dot(margin_rows, old[0], precision=lax.Precision.HIGHEST, preferred_element_type=F32)
    rotated[1] = jnp.dot(
        margin_rows * margin_rows, old[1], precision=lax.Precision.HIGHEST, preferred_element_type=F32
    )
    rot_copies = []
    for j in range(1, n_outer):
        copy = remote(
            rotated, rotated_in.at[j], rot_send.at[j], rot_recv.at[j], (lax.rem(z + j, n_outer), d)
        )
        copy.start()
        rot_copies.append(copy)

    load_own.wait()
    for copy in grad_copies:
        copy.wait_recv()
    total = grads[0].astype(F32)
    for j in range(1, n_dev):
        total = total + grads[j].astype(F32)
    high = total.astype(BF16)
    low = (total - high.astype(F32)).astype(BF16)
    both = jnp.concatenate([high, low], axis=1)
    for s in range(0, rank, width):
        part = contract_rows(basis[:, s : s + width], both)
        part = part[:, :cols] + part[:, cols:]
        projected[s // blk : (s + width) // blk] = part.reshape(width // blk, blk, cols)
    pairs = scatter_start(projected, projected_partner, pp_send, pp_recv)
    copies = scatter_middle(
        pairs, projected, projected_partner, projected_sum, projected_in, ps_send, ps_recv
    )
    block[...] = scatter_end(copies, projected_sum, projected_in)
    blk_copies = []
    for j in range(1, n_outer):
        copy = remote(
            block, block_in.at[j], blk_send.at[j], blk_recv.at[j], (lax.rem(z + j, n_outer), d)
        )
        copy.start()
        blk_copies.append(copy)
    for copy in rot_copies:
        copy.wait_recv()
    for copy in blk_copies:
        copy.wait_recv()

    first = rotated[0]
    second = rotated[1]
    proj = block[...]
    for j in range(1, n_outer):
        first = first + rotated_in[j, 0]
        second = second + rotated_in[j, 1]
        proj = proj + block_in[j]
    mean = beta_mean * first + (1.0 - beta_mean) * proj
    square = beta_square * second + (1.0 - beta_square) * proj * proj
    m_new[...] = mean
    v_new[...] = square
    direction[d] = (mean / bias_mean / (jnp.sqrt(square / bias_square) + adam_epsilon)).astype(BF16)
    dir_copies = []
    for j in range(1, n_dev):
        copy = remote(
            direction.at[d], direction.at[d], dir_send.at[j], dir_recv.at[j], (z, lax.rem(d + j, n_dev))
        )
        copy.start()
        dir_copies.append(copy)
    load_weight.wait()
    for copy in dir_copies:
        copy.wait_recv()
    directions = direction[...].reshape(rank, cols)
    tall = min(rows, 256)
    for s in range(0, rows, tall):
        update = jnp.dot(basis[s : s + tall, :], directions, preferred_element_type=F32)
        new_weight[s : s + tall, :] = weights[s : s + tall, :] - step_scale * update

    for k in range(per):
        owner = z * per + k
        mine = c == owner % 2

        @pl.when(d == owner)
        def _():
            for copy in moment_copies(k, owner):
                copy.wait_send()

        @pl.when(mine)
        def _():
            for i in range(2):
                remote(
                    moments.at[i, k], moments.at[i, k], fwd_send.at[i, k], fwd_recv.at[i, k], (z, partner)
                ).wait_send()

    for copy in grad_copies + rot_copies + blk_copies + dir_copies:
        copy.wait_send()
    for group in (margin_pairs, pairs):
        for _, _, copy in group:
            copy.wait_send()
    for group in (margin_copies, copies):
        for _, copy in group:
            copy.wait_send()


def on_device(n_outer, n_dev, partials, p_old, p_new, weight, m_old, v_old):
    rows, cols = weight.shape
    rank = p_new.shape[1]
    blk = rank // n_dev
    per = n_dev // n_outer
    span = per * blk
    n_chip = n_dev // 2
    p_old = lax.dynamic_slice_in_dim(p_old, lax.axis_index("outer") * span, span, axis=1)
    dma = pltpu.SemaphoreType.DMA
    anywhere = pl.BlockSpec(memory_space=pl.ANY)
    vmem = pl.BlockSpec(memory_space=pltpu.VMEM)
    return pl.pallas_call(
        functools.partial(kernel, n_outer, n_dev),
        out_shape=(
            jax.ShapeDtypeStruct((rows, cols), F32),
            jax.ShapeDtypeStruct((blk, cols), F32),
            jax.ShapeDtypeStruct((blk, cols), F32),
        ),
        in_specs=[anywhere] * 6,
        out_specs=(vmem, vmem, vmem),
        scratch_shapes=[
            pltpu.VMEM((n_dev, rows, cols), BF16),
            pltpu.VMEM((rows, rank), BF16),
            pltpu.VMEM((rows, span), BF16),
            pltpu.VMEM((rows, cols), F32),
            pltpu.VMEM((2, per, blk, cols), F32),
            pltpu.VMEM((n_dev, blk, span), F32),
            pltpu.VMEM((n_chip, blk, span), F32),
            pltpu.VMEM((n_chip, blk, span), F32),
            pltpu.VMEM((n_chip, blk, span), F32),
            pltpu.VMEM((2, blk, cols), F32),
            pltpu.VMEM((n_outer, 2, blk, cols), F32),
            pltpu.VMEM((n_dev, blk, cols), F32),
            pltpu.VMEM((n_chip, blk, cols), F32),
            pltpu.VMEM((n_chip, blk, cols), F32),
            pltpu.VMEM((n_chip, blk, cols), F32),
            pltpu.VMEM((blk, cols), F32),
            pltpu.VMEM((n_outer, blk, cols), F32),
            pltpu.VMEM((n_dev, blk, cols), BF16),
            dma((6,)),
            dma((n_dev,)),
            dma((n_dev,)),
            dma((2, per, n_chip)),
            dma((2, per)),
            dma((2, per)),
            dma((2, per)),
        ]
        + [dma((n_chip,))] * 4
        + [dma((n_outer,))] * 2
        + [dma((n_chip,))] * 4
        + [dma((n_outer,))] * 2
        + [dma((n_dev,))] * 2,
        compiler_params=pltpu.CompilerParams(
            collective_id=0, has_side_effects=True, vmem_limit_bytes=48 * 1024 * 1024
        ),
    )(partials[0], p_old, p_new, weight, m_old, v_old)


def solution(mesh):
    in_specs = (
        P(("outer", "dev"), None, None),
        P("dev", None),
        P("dev", None),
        P("dev", None),
        P("dev", None),
        P("dev", None),
    )
    out_specs = (P("dev", None), P("dev", None), P("dev", None))
    return jax.shard_map(
        functools.partial(on_device, mesh.shape["outer"], mesh.shape["dev"]),
        mesh=mesh,
        in_specs=in_specs,
        out_specs=out_specs,
        check_vma=False,
    )
```

time: 217 us -> 72.5 us (0.33)
  waiting for transfers between devices: 152 us -> 0 us
  Pallas kernels: 0 us -> 61.9 us
  blocking collectives: 28.8 us -> 0 us
  matrix products: 15 us -> 0 us
  between operations: 13.8 us -> 0.67 us
  local copies, waits for them, and re-layouts: 2.99 us -> 9.6 us
  other arithmetic: 3.94 us -> 0 us
    reduce_scatter x3 -> x0, waiting for transfers between devices: 115 us -> none  [the longest x1 54 us: on_device(): lax.psum_scatter(local_grad, 'dev', scatter_dimension=0, tiled=True)]
    pallas_call x0 -> x1, Pallas kernels: none -> 61.9 us  [on_device(): pl.pallas_call(functools.partial(kernel, n_outer, n_dev), out_shape=(jax....]
    psum x1 -> x0, waiting for transfers between devices: 36.5 us -> none  [on_device(): projected = lax.psum(projected, 'outer')]
    all_gather x3 -> x0, blocking collectives: 28.8 us -> none  [the longest x1 9.79 us: on_device(): second_piece = lax.all_gather(v_old, 'dev', axis=0, tiled=True)]
    dot_general x5 -> x0, matrix products: 15 us -> none  [the longest x1 5.92 us: on_device(): jnp.dot(columns.T, p_old, preferred_element_type=jnp.float32)]
    unnamed x14 -> x15, local copies, waits for them, and re-layouts: 2.99 us -> 9.53 us
    convert_element_type x1 -> x0, other arithmetic: 3.94 us -> none  [on_device(): local_grad = partials[0].astype(jnp.float32)]
  transfers between devices with their start and end apart: 4 -> 0, of which waited for: 4 -> 0; matrix products, arithmetic and copies ran while one was open for 3% -> 0% of each run, Pallas kernels for 0% -> 0%
where the time goes in v1:
time: 72.5 us; the launch traced here: 72.2 us
  Pallas kernels  61.9 us (85%)
  local copies, waits for them, and re-layouts  9.6 us (13%)
    pallas_call x1, Pallas kernels, on_device(): pl.pallas_call(functools.partial(kernel, n_outer, n_dev), out_shape=(jax....  61.9 us
    unnamed x15, local copies, waits for them, and re-layouts  9.53 us

profile of v1, /device:TPU:0, one launch (start us, length us, event | category | flops | bytes accessed | tf_op | source)
XLA Modules:
  0.0 72.2 jit_solution(2979155872987287462)
XLA Ops:
  0.6 0.0 copy-start
  0.6 1.6 %copy-done = bf16[1024,1024]{1,0:T(8,128)(2,1)S(1)} copy-done((bf16[1024,1024]{1,0:T(8,128)(2,1)S(1)}, bf16[1024,1024]{1,0:T(8,128)(2,1)}, u32[]{:S(2)}) %copy-start) | copy-done | bytes 2097176
  2.2 0.1 constant_dynamic-slice_fusion.p_old
  2.3 0.0 copy-start.1
  2.3 1.6 %copy-done.1 = bf16[1,8192,128]{2,1,0:T(8,128)(2,1)S(1)} copy-done((bf16[1,8192,128]{2,1,0:T(8,128)(2,1)S(1)}, bf16[1,8192,128]{2,1,0:T(8,128)(2,1)}, u32[]{:S(2)}) %copy-start.1) | copy-done | bytes 2097176
  3.9 0.0 copy-start.2
  3.9 1.6 %copy-done.2 = bf16[1024,1024]{1,0:T(8,128)(2,1)S(1)} copy-done((bf16[1024,1024]{1,0:T(8,128)(2,1)S(1)}, bf16[1024,1024]{1,0:T(8,128)(2,1)}, u32[]{:S(2)}) %copy-start.2) | copy-done | bytes 2097176
  5.5 0.0 copy-start.3
  5.5 1.0 %copy-done.3 = f32[1024,128]{1,0:T(8,128)S(1)} copy-done((f32[1024,128]{1,0:T(8,128)S(1)}, f32[1024,128]{1,0:T(8,128)}, u32[]{:S(2)}) %copy-start.3) | copy-done | bytes 524312
  6.5 0.0 copy-start.4
  6.5 0.8 %copy-done.4 = f32[128,128]{1,0:T(8,128)S(1)} copy-done((f32[128,128]{1,0:T(8,128)S(1)}, f32[128,128]{1,0:T(8,128)}, u32[]{:S(2)}) %copy-start.4) | copy-done | bytes 65560
  7.4 0.0 copy-start.5
  7.4 0.8 %copy-done.5 = f32[128,128]{1,0:T(8,128)S(1)} copy-done((f32[128,128]{1,0:T(8,128)S(1)}, f32[128,128]{1,0:T(8,128)}, u32[]{:S(2)}) %copy-start.5) | copy-done | bytes 65560
  8.2 61.9 %shard_map.85 = (f32[1024,128]{1,0:T(8,128)S(1)}, f32[128,128]{1,0:T(8,128)S(1)}, f32[128,128]{1,0:T(8,128)S(1)}) custom-call(bf16[8192,128]{1,0:T(8,128)(2,1)S(1)} %bitcast.1, bf16[1024,256]{1,0:T(8,128)(2,1)S(1)} %constant_dynamic-slice_fusion.p_old, bf16[1024,1024]{1,0:T(8,128)(2,1)S(1)} %copy-done.2, f32[1024,128]{1,0:T(8,128)S(1)} %copy-done.3, ...), custom_call_target="tpu_custom_call" | custom-call | tf_op jit(solution)/shard_map/pallas_call | solution.py:324
  70.1 0.8 %copy.12 = f32[1024,128]{1,0:T(8,128)} copy(f32[1024,128]{1,0:T(8,128)S(1)} %get-tuple-element.6) | data formatting | bytes 1048576
  70.9 0.6 copy.13
  71.5 0.6 copy.14
Async XLA Ops:
  0.6 1.6 %copy-start = (bf16[1024,1024]{1,0:T(8,128)(2,1)S(1)}, bf16[1024,1024]{1,0:T(8,128)(2,1)}, u32[]{:S(2)}) copy-start(bf16[1024,1024]{1,0:T(8,128)(2,1)} %param.7) | copy-start | bytes 6291460
  2.3 1.6 %copy-start.1 = (bf16[1,8192,128]{2,1,0:T(8,128)(2,1)S(1)}, bf16[1,8192,128]{2,1,0:T(8,128)(2,1)}, u32[]{:S(2)}) copy-start(bf16[1,8192,128]{2,1,0:T(8,128)(2,1)} %param.6) | copy-start | bytes 6291460
  3.9 1.6 %copy-start.2 = (bf16[1024,1024]{1,0:T(8,128)(2,1)S(1)}, bf16[1024,1024]{1,0:T(8,128)(2,1)}, u32[]{:S(2)}) copy-start(bf16[1024,1024]{1,0:T(8,128)(2,1)} %p_new.1) | copy-start | bytes 6291460
  5.5 1.0 %copy-start.3 = (f32[1024,128]{1,0:T(8,128)S(1)}, f32[1024,128]{1,0:T(8,128)}, u32[]{:S(2)}) copy-start(f32[1024,128]{1,0:T(8,128)} %weight.1) | copy-start | bytes 1572868
  6.5 0.8 %copy-start.4 = (f32[128,128]{1,0:T(8,128)S(1)}, f32[128,128]{1,0:T(8,128)}, u32[]{:S(2)}) copy-start(f32[128,128]{1,0:T(8,128)} %m_old.1) | copy-start | bytes 196612
  7.4 0.8 %copy-start.5 = (f32[128,128]{1,0:T(8,128)S(1)}, f32[128,128]{1,0:T(8,128)}, u32[]{:S(2)}) copy-start(f32[128,128]{1,0:T(8,128)} %v_old.1) | copy-start | bytes 196612

commit v2 on v1

--- a/solution.py
+++ b/solution.py
@@ -13,6 +13,10 @@
 bias_square = 0.9940794707796659
 adam_epsilon = 1e-08
 step_scale = 0.5
+
+chunks = 2
+vmem_limit = 67043328
+finish_limit = 67043328
 
 MESH = pl.DeviceIdType.MESH
 F32 = jnp.float32
@@ -54,6 +58,7 @@
     block_in,
     direction,
     load_sem,
+    old_sem,
     grad_send,
     grad_recv,
     mom_send,
@@ -99,8 +104,19 @@
 
     load_new = pltpu.make_async_copy(p_new, basis, load_sem.at[0])
     load_new.start()
-    load_old = pltpu.make_async_copy(p_old, basis_old, load_sem.at[1])
-    load_old.start()
+    if p_old.shape[1] == per * blk:
+        old_loads = [pltpu.make_async_copy(p_old, basis_old, old_sem.at[0])]
+    else:
+        old_loads = [
+            pltpu.make_async_copy(
+                p_old.at[:, pl.ds(pl.multiple_of((k * n_outer + z) * blk, blk), blk)],
+                basis_old.at[:, k * blk : (k + 1) * blk],
+                old_sem.at[k],
+            )
+            for k in range(per)
+        ]
+    for load in old_loads:
+        load.start()
     load_weight = pltpu.make_async_copy(weight, weights, load_sem.at[2])
     load_weight.start()
     load_own = pltpu.make_async_copy(
@@ -119,7 +135,7 @@
         return copies
 
     for k in range(per):
-        owner = z * per + k
+        owner = k * n_outer + z
 
         @pl.when(d == owner)
         def _():
@@ -128,21 +144,28 @@
             for i, src in enumerate((m_old, v_old)):
                 pltpu.make_async_copy(src, moments.at[i, k], load_sem.at[4 + i]).start()
 
-    grad_copies = []
-    for j in range(1, n_dev):
-        to = lax.rem(d + j, n_dev)
-        copy = remote(
-            partials.at[pl.ds(pl.multiple_of(to * rows, rows), rows)],
-            grads.at[j],
-            grad_send.at[j],
-            grad_recv.at[j],
-            (z, to),
-        )
-        copy.start()
-        grad_copies.append(copy)
+    tall = rows // chunks
+
+    def send_gradients(chunk):
+        copies = []
+        for j in range(1, n_dev):
+            to = lax.rem(d + j, n_dev)
+            copy = remote(
+                partials.at[pl.ds(pl.multiple_of(to * rows + chunk * tall, tall), tall)],
+                grads.at[j, chunk * tall : (chunk + 1) * tall],
+                grad_send.at[chunk, j],
+                grad_recv.at[chunk, j],
+                (z, to),
+            )
+            copy.start()
+            copies.append(copy)
+        return copies
+
+    grad_copies = [send_gradients(0)]
 
     load_new.wait()
-    load_old.wait()
+    for load in old_loads:
+        load.wait()
     width = min(rank, 256)
     for s in range(0, rank, width):
         part = contract_rows(basis[:, s : s + width], basis_old[...])
@@ -178,7 +201,7 @@
     margin_pairs = scatter_start(margin, margin_partner, mp_send, mp_recv)
 
     for k in range(per):
-        owner = z * per + k
+        owner = k * n_outer + z
         mine = c == owner % 2
 
         @pl.when(d == owner)
@@ -202,8 +225,11 @@
         margin_pairs, margin, margin_partner, margin_sum, margin_in, ms_send, ms_recv
     )
 
+    for chunk in range(1, chunks):
+        grad_copies.append(send_gradients(chunk))
+
     for k in range(per):
-        mine = c == (z * per + k) % 2
+        mine = c == (k * n_outer + z) % 2
 
         @pl.when(jnp.logical_not(mine))
         def _():
@@ -227,18 +253,21 @@
         rot_copies.append(copy)
 
     load_own.wait()
-    for copy in grad_copies:
-        copy.wait_recv()
-    total = grads[0].astype(F32)
-    for j in range(1, n_dev):
-        total = total + grads[j].astype(F32)
-    high = total.astype(BF16)
-    low = (total - high.astype(F32)).astype(BF16)
-    both = jnp.concatenate([high, low], axis=1)
-    for s in range(0, rank, width):
-        part = contract_rows(basis[:, s : s + width], both)
-        part = part[:, :cols] + part[:, cols:]
-        projected[s // blk : (s + width) // blk] = part.reshape(width // blk, blk, cols)
+    for chunk in range(chunks):
+        for copy in grad_copies[chunk]:
+            copy.wait_recv()
+        part_rows = slice(chunk * tall, (chunk + 1) * tall)
+        total = grads[0, part_rows].astype(F32)
+        for j in range(1, n_dev):
+            total = total + grads[j, part_rows].astype(F32)
+        high = total.astype(BF16)
+        low = (total - high.astype(F32)).astype(BF16)
+        both = jnp.concatenate([high, low], axis=1)
+        for s in range(0, rank, width):
+            part = contract_rows(basis[part_rows, s : s + width], both)
+            part = (part[:, :cols] + part[:, cols:]).reshape(width // blk, blk, cols)
+            blocks = slice(s // blk, (s + width) // blk)
+            projected[blocks] = part if chunk == 0 else projected[blocks] + part
     pairs = scatter_start(projected, projected_partner, pp_send, pp_recv)
     copies = scatter_middle(
         pairs, projected, projected_partner, projected_sum, projected_in, ps_send, ps_recv
@@ -285,7 +314,7 @@
         new_weight[s : s + tall, :] = weights[s : s + tall, :] - step_scale * update
 
     for k in range(per):
-        owner = z * per + k
+        owner = k * n_outer + z
         mine = c == owner % 2
 
         @pl.when(d == owner)
@@ -300,7 +329,7 @@
                     moments.at[i, k], moments.at[i, k], fwd_send.at[i, k], fwd_recv.at[i, k], (z, partner)
                 ).wait_send()
 
-    for copy in grad_copies + rot_copies + blk_copies + dir_copies:
+    for copy in sum(grad_copies, []) + rot_copies + blk_copies + dir_copies:
         copy.wait_send()
     for group in (margin_pairs, pairs):
         for _, _, copy in group:
@@ -310,6 +339,12 @@
             copy.wait_send()
 
 
+def hand_over(weight_in, m_in, v_in, weight_out, m_out, v_out):
+    weight_out[...] = weight_in[...]
+    m_out[...] = m_in[...]
+    v_out[...] = v_in[...]
+
+
 def on_device(n_outer, n_dev, partials, p_old, p_new, weight, m_old, v_old):
     rows, cols = weight.shape
     rank = p_new.shape[1]
@@ -317,11 +352,19 @@
     per = n_dev // n_outer
     span = per * blk
     n_chip = n_dev // 2
-    p_old = lax.dynamic_slice_in_dim(p_old, lax.axis_index("outer") * span, span, axis=1)
+    if blk % 128:
+        z = lax.axis_index("outer")
+        p_old = jnp.concatenate(
+            [
+                lax.dynamic_slice_in_dim(p_old, (k * n_outer + z) * blk, blk, axis=1)
+                for k in range(per)
+            ],
+            axis=1,
+        )
     dma = pltpu.SemaphoreType.DMA
-    anywhere = pl.BlockSpec(memory_space=pl.ANY)
+    anywhere = pl.BlockSpec(memory_space=pltpu.HBM)
     vmem = pl.BlockSpec(memory_space=pltpu.VMEM)
-    return pl.pallas_call(
+    results = pl.pallas_call(
         functools.partial(kernel, n_outer, n_dev),
         out_shape=(
             jax.ShapeDtypeStruct((rows, cols), F32),
@@ -350,8 +393,9 @@
             pltpu.VMEM((n_outer, blk, cols), F32),
             pltpu.VMEM((n_dev, blk, cols), BF16),
             dma((6,)),
-            dma((n_dev,)),
-            dma((n_dev,)),
+            dma((per,)),
+            dma((chunks, n_dev)),
+            dma((chunks, n_dev)),
             dma((2, per, n_chip)),
             dma((2, per)),
             dma((2, per)),
@@ -363,9 +407,16 @@
         + [dma((n_outer,))] * 2
         + [dma((n_dev,))] * 2,
         compiler_params=pltpu.CompilerParams(
-            collective_id=0, has_side_effects=True, vmem_limit_bytes=48 * 1024 * 1024
+            collective_id=0, has_side_effects=True, vmem_limit_bytes=vmem_limit
         ),
     )(partials[0], p_old, p_new, weight, m_old, v_old)
+    return pl.pallas_call(
+        hand_over,
+        out_shape=tuple(jax.ShapeDtypeStruct(r.shape, r.dtype) for r in results),
+        in_specs=[vmem] * 3,
+        out_specs=(vmem,) * 3,
+        compiler_params=pltpu.CompilerParams(vmem_limit_bytes=finish_limit),
+    )(*results)
 
 
 def solution(mesh):

time: 72.5 us -> 58.6 us (0.81)
  local copies, waits for them, and re-layouts: 9.6 us -> 0 us
  Pallas kernels: 61.9 us -> 57.8 us
    unnamed x15 -> x0, local copies, waits for them, and re-layouts: 9.53 us -> none
    pallas_call x1, Pallas kernels: 61.9 us -> 55.9 us  [on_device(): pl.pallas_call(functools.partial(kernel, n_outer, n_dev), out_shape=(jax....]
    pallas_call x0 -> x1, Pallas kernels: none -> 1.93 us  [on_device(): pl.pallas_call(hand_over, out_shape=tuple((jax.ShapeDtypeStruct(r.shape,...]
where the time goes in v2:
time: 58.6 us; the launch traced here: 58.5 us
  Pallas kernels  57.8 us (99%)
  between operations  0.64 us (1%)
    pallas_call x1, Pallas kernels, on_device(): pl.pallas_call(functools.partial(kernel, n_outer, n_dev), out_shape=(jax....  55.9 us
    pallas_call x1, Pallas kernels, on_device(): pl.pallas_call(hand_over, out_shape=tuple((jax.ShapeDtypeStruct(r.shape,...  1.93 us

profile of v2, /device:TPU:0, one launch (start us, length us, event | category | flops | bytes accessed | tf_op | source)
XLA Modules:
  0.0 58.5 jit_solution(78066884299946711)
XLA Ops:
  0.6 55.9 %shard_map.85 = (f32[1024,128]{1,0:T(8,128)}, f32[128,128]{1,0:T(8,128)}, f32[128,128]{1,0:T(8,128)}) custom-call(bf16[8192,128]{1,0:T(8,128)(2,1)} %bitcast.1, bf16[1024,1024]{1,0:T(8,128)(2,1)} %p_old.1, bf16[1024,1024]{1,0:T(8,128)(2,1)} %p_new.1, f32[1024,128]{1,0:T(8,128)} %weight.1, f32[128,128]{1,0:T(8,128)} %m_old.1, f32[128,128]{1,0:T(8,128)} %v_old.1), custom_call_target="tpu_custom_call" | custom-call | tf_op jit(solution)/shard_map/pallas_call | solution.py:367
  56.5 1.9 %shard_map.86 = (f32[1024,128]{1,0:T(8,128)}, f32[128,128]{1,0:T(8,128)}, f32[128,128]{1,0:T(8,128)}) custom-call(f32[1024,128]{1,0:T(8,128)} %get-tuple-element.6.weight_in, f32[128,128]{1,0:T(8,128)} %get-tuple-element.7.m_in, f32[128,128]{1,0:T(8,128)} %get-tuple-element.8.v_in), custom_call_target="tpu_custom_call" | custom-call | tf_op jit(solution)/shard_map/pallas_call | solution.py:413

commit v3 on v2

--- a/solution.py
+++ b/solution.py
@@ -15,6 +15,8 @@
 step_scale = 0.5
 
 chunks = 2
+early = 1
+parts = 2
 vmem_limit = 67043328
 finish_limit = 67043328
 
@@ -79,6 +81,15 @@
     blk_recv,
     dir_send,
     dir_recv,
+    own_terms,
+    pair_terms,
+    far_sum,
+    relay_in,
+    merged,
+    merged_in,
+    own_sem,
+    hop_send,
+    hop_recv,
 ):
     z = lax.axis_index("outer")
     d = lax.axis_index("dev")
@@ -161,7 +172,49 @@
             copies.append(copy)
         return copies
 
-    grad_copies = [send_gradients(0)]
+    relayed = n_chip == 4
+    hop_copies = []
+
+    def hop(i, src, dst, to):
+        copy = remote(src, dst, hop_send.at[i], hop_recv.at[i], (z, to))
+        copy.start()
+        hop_copies.append(copy)
+        return copy
+
+    def rows_of(to, offset, count):
+        return partials.at[pl.ds(pl.multiple_of(to * rows + offset, tall), count)]
+
+    if relayed:
+        side = q + 1 - 2 * (q % 2)
+        over = lax.rem(q + 2, 4)
+        far = lax.rem(side + 2, 4)
+        regions = ((far, 0, rows, 0), (over, 0, tall, rows), (side, tall, tall, rows + tall))
+        pair_copies, own_loads = [], []
+        for i, (chip, offset, count, place) in enumerate(regions):
+            at = slice(place, place + count)
+            pair_copies.append(hop(i, rows_of(2 * chip + 1 - c, offset, count), pair_terms.at[at], partner))
+            load = pltpu.make_async_copy(
+                rows_of(2 * chip + c, offset, count), own_terms.at[at], own_sem.at[i]
+            )
+            load.start()
+            own_loads.append(load)
+        direct = []
+        for h, chip in enumerate((side, over)):
+            at = slice(h * tall, (h + 1) * tall)
+            for r in range(2):
+                to = 2 * chip + (c if r == 0 else 1 - c)
+                direct.append(hop(3 + 2 * h + r, rows_of(to, h * tall, tall), grads.at[2 + r, at], to))
+        near = hop(7, rows_of(partner, 0, rows), grads.at[1], partner)
+        pair_copies[0].wait_recv()
+        own_loads[0].wait()
+        far_sum[...] = own_terms[:rows].astype(F32) + pair_terms[:rows].astype(F32)
+        relays = [
+            hop(8 + h, far_sum.at[h * tall : (h + 1) * tall], relay_in.at[h], 2 * chip + c)
+            for h, chip in enumerate((side, over))
+        ]
+        grad_copies = []
+    else:
+        grad_copies = [send_gradients(chunk) for chunk in range(early)]
 
     load_new.wait()
     for load in old_loads:
@@ -225,8 +278,18 @@
         margin_pairs, margin, margin_partner, margin_sum, margin_in, ms_send, ms_recv
     )
 
-    for chunk in range(1, chunks):
-        grad_copies.append(send_gradients(chunk))
+    if relayed:
+        passed = []
+        for h, chip in enumerate((over, side)):
+            at = slice(rows + h * tall, rows + (h + 1) * tall)
+            pair_copies[1 + h].wait_recv()
+            own_loads[1 + h].wait()
+            relays[h].wait_recv()
+            merged[h] = own_terms[at].astype(F32) + pair_terms[at].astype(F32) + relay_in[h]
+            passed.append(hop(10 + h, merged.at[h], merged_in.at[h], 2 * chip + c))
+    else:
+        for chunk in range(early, chunks):
+            grad_copies.append(send_gradients(chunk))
 
     for k in range(per):
         mine = c == (k * n_outer + z) % 2
@@ -254,12 +317,20 @@
 
     load_own.wait()
     for chunk in range(chunks):
-        for copy in grad_copies[chunk]:
-            copy.wait_recv()
+        if relayed:
+            if chunk == 0:
+                near.wait_recv()
+            for copy in direct[2 * chunk : 2 * chunk + 2] + [passed[chunk]]:
+                copy.wait_recv()
+        else:
+            for copy in grad_copies[chunk]:
+                copy.wait_recv()
         part_rows = slice(chunk * tall, (chunk + 1) * tall)
         total = grads[0, part_rows].astype(F32)
-        for j in range(1, n_dev):
+        for j in range(1, 4 if relayed else n_dev):
             total = total + grads[j, part_rows].astype(F32)
+        if relayed:
+            total = total + merged_in[chunk]
         high = total.astype(BF16)
         low = (total - high.astype(F32)).astype(BF16)
         both = jnp.concatenate([high, low], axis=1)
@@ -268,42 +339,65 @@
             part = (part[:, :cols] + part[:, cols:]).reshape(width // blk, blk, cols)
             blocks = slice(s // blk, (s + width) // blk)
             projected[blocks] = part if chunk == 0 else projected[blocks] + part
-    pairs = scatter_start(projected, projected_partner, pp_send, pp_recv)
-    copies = scatter_middle(
-        pairs, projected, projected_partner, projected_sum, projected_in, ps_send, ps_recv
-    )
-    block[...] = scatter_end(copies, projected_sum, projected_in)
+    half = blk // parts
+    views = [slice(h * half, (h + 1) * half) for h in range(parts)]
+    pairs = [
+        scatter_start(projected.at[:, v], projected_partner.at[:, v], pp_send.at[h], pp_recv.at[h])
+        for h, v in enumerate(views)
+    ]
+    copies = [
+        scatter_middle(
+            pairs[h],
+            projected.at[:, v],
+            projected_partner.at[:, v],
+            projected_sum.at[:, v],
+            projected_in.at[:, v],
+            ps_send.at[h],
+            ps_recv.at[h],
+        )
+        for h, v in enumerate(views)
+    ]
     blk_copies = []
-    for j in range(1, n_outer):
-        copy = remote(
-            block, block_in.at[j], blk_send.at[j], blk_recv.at[j], (lax.rem(z + j, n_outer), d)
-        )
-        copy.start()
-        blk_copies.append(copy)
+    for h, v in enumerate(views):
+        block[v] = scatter_end(copies[h], projected_sum.at[:, v], projected_in.at[:, v])
+        for j in range(1, n_outer):
+            copy = remote(
+                block.at[v],
+                block_in.at[j, v],
+                blk_send.at[h, j],
+                blk_recv.at[h, j],
+                (lax.rem(z + j, n_outer), d),
+            )
+            copy.start()
+            blk_copies.append(copy)
     for copy in rot_copies:
         copy.wait_recv()
-    for copy in blk_copies:
-        copy.wait_recv()
-
-    first = rotated[0]
-    second = rotated[1]
-    proj = block[...]
-    for j in range(1, n_outer):
-        first = first + rotated_in[j, 0]
-        second = second + rotated_in[j, 1]
-        proj = proj + block_in[j]
-    mean = beta_mean * first + (1.0 - beta_mean) * proj
-    square = beta_square * second + (1.0 - beta_square) * proj * proj
-    m_new[...] = mean
-    v_new[...] = square
-    direction[d] = (mean / bias_mean / (jnp.sqrt(square / bias_square) + adam_epsilon)).astype(BF16)
     dir_copies = []
-    for j in range(1, n_dev):
-        copy = remote(
-            direction.at[d], direction.at[d], dir_send.at[j], dir_recv.at[j], (z, lax.rem(d + j, n_dev))
-        )
-        copy.start()
-        dir_copies.append(copy)
+    for h, v in enumerate(views):
+        for copy in blk_copies[h * (n_outer - 1) : (h + 1) * (n_outer - 1)]:
+            copy.wait_recv()
+        first = rotated[0, v]
+        second = rotated[1, v]
+        proj = block[v]
+        for j in range(1, n_outer):
+            first = first + rotated_in[j, 0, v]
+            second = second + rotated_in[j, 1, v]
+            proj = proj + block_in[j, v]
+        mean = beta_mean * first + (1.0 - beta_mean) * proj
+        square = beta_square * second + (1.0 - beta_square) * proj * proj
+        m_new[v] = mean
+        v_new[v] = square
+        direction[d, v] = (mean / bias_mean / (jnp.sqrt(square / bias_square) + adam_epsilon)).astype(BF16)
+        for j in range(1, n_dev):
+            copy = remote(
+                direction.at[d, v],
+                direction.at[d, v],
+                dir_send.at[h, j],
+                dir_recv.at[h, j],
+                (z, lax.rem(d + j, n_dev)),
+            )
+            copy.start()
+            dir_copies.append(copy)
     load_weight.wait()
     for copy in dir_copies:
         copy.wait_recv()
@@ -329,12 +423,12 @@
                     moments.at[i, k], moments.at[i, k], fwd_send.at[i, k], fwd_recv.at[i, k], (z, partner)
                 ).wait_send()
 
-    for copy in sum(grad_copies, []) + rot_copies + blk_copies + dir_copies:
+    for copy in hop_copies + sum(grad_copies, []) + rot_copies + blk_copies + dir_copies:
         copy.wait_send()
-    for group in (margin_pairs, pairs):
+    for group in [margin_pairs] + pairs:
         for _, _, copy in group:
             copy.wait_send()
-    for group in (margin_copies, copies):
+    for group in [margin_copies] + copies:
         for _, copy in group:
             copy.wait_send()
 
@@ -403,9 +497,20 @@
         ]
         + [dma((n_chip,))] * 4
         + [dma((n_outer,))] * 2
-        + [dma((n_chip,))] * 4
-        + [dma((n_outer,))] * 2
-        + [dma((n_dev,))] * 2,
+        + [dma((parts, n_chip))] * 4
+        + [dma((parts, n_outer))] * 2
+        + [dma((parts, n_dev))] * 2
+        + [
+            pltpu.VMEM((2 * rows, cols), BF16),
+            pltpu.VMEM((2 * rows, cols), BF16),
+            pltpu.VMEM((rows, cols), F32),
+            pltpu.VMEM((2, rows // 2, cols), F32),
+            pltpu.VMEM((2, rows // 2, cols), F32),
+            pltpu.VMEM((2, rows // 2, cols), F32),
+            dma((3,)),
+            dma((12,)),
+            dma((12,)),
+        ],
         compiler_params=pltpu.CompilerParams(
             collective_id=0, has_side_effects=True, vmem_limit_bytes=vmem_limit
         ),

time: 58.6 us -> 53.9 us (0.920)
  Pallas kernels: 57.8 us -> 53.1 us
    pallas_call x1, Pallas kernels: 55.9 us -> 51.2 us  [on_device(): pl.pallas_call(functools.partial(kernel, n_outer, n_dev), out_shape=(jax....]
where the time goes in v3:
time: 53.9 us; the launch traced here: 53.8 us
  Pallas kernels  53.1 us (99%)
  between operations  0.64 us (1%)
    pallas_call x1, Pallas kernels, on_device(): pl.pallas_call(functools.partial(kernel, n_outer, n_dev), out_shape=(jax....  51.2 us
    pallas_call x1, Pallas kernels, on_device(): pl.pallas_call(hand_over, out_shape=tuple((jax.ShapeDtypeStruct(r.shape,...  1.93 us

profile of v3, /device:TPU:0, one launch (start us, length us, event | category | flops | bytes accessed | tf_op | source)
XLA Modules:
  0.0 53.8 jit_solution(17043605253378285092)
XLA Ops:
  0.6 51.2 %shard_map.85 = (f32[1024,128]{1,0:T(8,128)}, f32[128,128]{1,0:T(8,128)}, f32[128,128]{1,0:T(8,128)}) custom-call(bf16[8192,128]{1,0:T(8,128)(2,1)} %bitcast.1, bf16[1024,1024]{1,0:T(8,128)(2,1)} %p_old.1, bf16[1024,1024]{1,0:T(8,128)(2,1)} %p_new.1, f32[1024,128]{1,0:T(8,128)} %weight.1, f32[128,128]{1,0:T(8,128)} %m_old.1, f32[128,128]{1,0:T(8,128)} %v_old.1), custom_call_target="tpu_custom_call" | custom-call | tf_op jit(solution)/shard_map/pallas_call | solution.py:461
  51.9 1.9 %shard_map.86 = (f32[1024,128]{1,0:T(8,128)}, f32[128,128]{1,0:T(8,128)}, f32[128,128]{1,0:T(8,128)}) custom-call(f32[1024,128]{1,0:T(8,128)} %get-tuple-element.6.weight_in, f32[128,128]{1,0:T(8,128)} %get-tuple-element.7.m_in, f32[128,128]{1,0:T(8,128)} %get-tuple-element.8.v_in), custom_call_target="tpu_custom_call" | custom-call | tf_op jit(solution)/shard_map/pallas_call | solution.py:518
